TPU v7x, 32 devices: a whole 2x2x4 slice. The times are simulated.
32 devices in a mesh: space: 8 (over y, x, core), members: 4 (over z).
Axes of the slice: x: 2, y: 2, z: 4, core: 2. Of those that a mesh axis runs over, the one named last changes fastest.
Arguments:
- ensemble: bfloat16 [128, 65536], P('members', 'space'), may hold values from -6 to 6
- op_blocks: bfloat16 [512, 3, 128, 128], P('space'), may hold values from -0.3125 to 0.3125
- col_index: int32 [512, 2], P('space'), may hold values from 0 to 511, as said below
- weights: float32 [128, 512], P('members', 'space')
- innovations: float32 [2, 65536], P(None, 'space'), may hold values from -6 to 6
- obs_precision: float32 [2, 65536], P(None, 'space'), may hold values from 0.25 to 4
Outputs:
- grad_ens: float32 [128, 65536], P('members', 'space')
- direction: float32 [128, 512], P('members', 'space')
Inputs may be any that keep to these rules, and one draw needn't show every extreme that they name: col_index[r, 0] lies in [r - 32, r - 1] and col_index[r, 1] in [r + 1, r + 32], each clipped to the grid; in every aligned run of 64 block-rows some row reaches back by exactly 32 and some row forward by exactly 32, before clipping.
All inputs are finite; a program needn't handle non-finite values.
Results may differ from a plain program's by a relative error of at most 0.011.
Values may be sent and summed in bfloat16 or wider, within the bound.
No kernel may reach another device: no remote copies, remote signals or barrier semaphores. Data moves between devices by JAX's collectives and lax.ppermute only.
A program may use at most 64 MiB of HBM per device.

v0:
```python
import jax
import jax.numpy as jnp
from jax import lax
from jax.sharding import PartitionSpec as P

MEMBERS = 128


def padded(x, sides, width):
    for axis, dim in sides:
        devices, length = (lax.axis_size(axis), x.shape[dim])
        up = [(i, (i + 1) % devices) for i in range(devices - 1)]
        down = [(j, i) for i, j in up]
        last = lax.slice_in_dim(x, length - width, length, axis=dim)
        leading = lax.slice_in_dim(x, 0, width, axis=dim)
        before = lax.ppermute(last, axis, up)
        after = lax.ppermute(leading, axis, down)
        x = jnp.concatenate([before, x, after], axis=dim)
    return x


def on_device(ensemble, op_blocks, col_index, weights, innovations, obs_precision):
    member_count = ensemble.shape[0]
    blocks = op_blocks.shape[0]
    per_row = op_blocks.shape[1]
    block_size = op_blocks.shape[2]
    offset_rows = lax.axis_index("space") * blocks - blocks
    local_cols = col_index - offset_rows
    own_rows = (jnp.arange(blocks, dtype=jnp.int32) + blocks)[:, None]
    every_col = jnp.concatenate([own_rows, local_cols], axis=1)
    wide_rows = blocks + 2 * blocks

    def widen_halo(flat_values):
        widened = padded(flat_values, (("space", 1),), blocks * block_size)
        return widened.reshape(member_count, wide_rows, block_size)

    def forward(values_in):
        flat_values = values_in.reshape(member_count, blocks * block_size)
        widened = widen_halo(flat_values)
        picked = widened[:, every_col, :]
        return jnp.einsum("rkij,mrkj->mri", op_blocks, picked, preferred_element_type=jnp.float32)

    def adjoint(cotangent):
        contributions = jnp.einsum(
            "rkij,mri->mrkj", op_blocks, cotangent, preferred_element_type=jnp.float32
        )
        spread_rows = jnp.zeros((member_count, wide_rows, block_size), jnp.float32)
        spread_rows = spread_rows.at[:, every_col.reshape(-1), :].add(
            contributions.reshape(member_count, blocks * per_row, block_size)
        )
        outer_rims = jnp.concatenate(
            [spread_rows[:, :blocks], spread_rows[:, blocks + blocks :]], axis=1
        )
        outer_rims = outer_rims.reshape(member_count, 2 * blocks * block_size)
        received = padded(outer_rims, (("space", 1),), blocks * block_size)
        received = received.reshape(member_count, 4 * blocks, block_size)
        own_sums = spread_rows[:, blocks : blocks + blocks]
        own_sums = own_sums.at[:, :blocks].add(received[:, :blocks])
        own_sums = own_sums.at[:, blocks - blocks :].add(received[:, 3 * blocks :])
        return own_sums

    states = ensemble.reshape(member_count, blocks, block_size)
    prop_one = forward(states).astype(jnp.bfloat16)
    prop_two = forward(prop_one).astype(jnp.bfloat16)
    member_scale = (MEMBERS - 1) ** (-0.5)
    weight_col = weights[:, :, None]
    partial_sums = jnp.stack(
        [
            jnp.sum(weight_col * prop_one.astype(jnp.float32), axis=0),
            jnp.sum(weight_col * prop_two.astype(jnp.float32), axis=0),
        ]
    )
    observed = innovations.reshape(2, blocks, block_size)
    precision = obs_precision.reshape(2, blocks, block_size)
    increments = lax.psum(partial_sums, "members") * member_scale
    residual = precision * (increments - observed)
    cot_one = (member_scale * weight_col * residual[0][None]).astype(jnp.bfloat16)
    cot_two = (member_scale * weight_col * residual[1][None]).astype(jnp.bfloat16)
    adjoint_mid = (cot_one.astype(jnp.float32) + adjoint(cot_two)).astype(jnp.bfloat16)
    grad_ens = adjoint(adjoint_mid).reshape(member_count, blocks * block_size)
    products = (
        prop_one.astype(jnp.float32) * residual[0][None]
        + prop_two.astype(jnp.float32) * residual[1][None]
    )
    grad_weights = weights + member_scale * jnp.sum(products, axis=2)
    squares = lax.psum(jnp.sum(grad_weights * grad_weights, axis=1), "space")
    mean_square = squares / (blocks * lax.axis_size("space"))
    direction = grad_weights / jnp.sqrt(mean_square + 1e-06)[:, None]
    return (grad_ens, direction)


def solution(mesh):
    placed = (
        P("members", "space"),
        P("space", None, None, None),
        P("space", None),
        P("members", "space"),
        P(None, "space"),
        P(None, "space"),
    )
    return jax.shard_map(
        on_device,
        mesh=mesh,
        in_specs=placed,
        out_specs=(P("members", "space"), P("members", "space")),
        check_vma=False,
    )
```

profile of v0, /device:TPU:1, one launch (start us, length us, event | category | flops | bytes accessed | tf_op | source)
XLA Modules:
  0.0 225.6 jit_solution(5958671020050633099)
XLA Ops:
  7.2 4.5 %collective-permute-start = (bf16[32,8192]{1,0:T(8,128)(2,1)}, bf16[32,8192]{1,0:T(8,128)(2,1)S(1)}, u32[]{:S(2)}, u32[]{:S(2)}) collective-permute-start(bf16[32,8192]{1,0:T(8,128)(2,1)} %param.22), channel_id=1, source_target_pairs={{0,4},{4,8},{8,12},{12,16},{16,20},{20,24},{24,28},{1,5},{5,9},{9,... | collective-permute-start | bytes 1572872 | tf_op jit(solution)/shard_map/ppermute | solution.py:16
  11.7 1.9 collective-permute-start.1
  14.6 3.5 %collective-permute-done = bf16[32,8192]{1,0:T(8,128)(2,1)S(1)} collective-permute-done((bf16[32,8192]{1,0:T(8,128)(2,1)}, bf16[32,8192]{1,0:T(8,128)(2,1)S(1)}, u32[]{:S(2)}, u32[]{:S(2)}) %collective-permute-start) | collective-permute-done | bytes 524320 | tf_op jit(solution)/shard_map/ppermute | solution.py:16
  18.1 7.2 %collective-permute-done.1 = bf16[32,8192]{1,0:T(8,128)(2,1)S(1)} collective-permute-done((bf16[32,8192]{1,0:T(8,128)(2,1)}, bf16[32,8192]{1,0:T(8,128)(2,1)S(1)}, u32[]{:S(2)}, u32[]{:S(2)}) %collective-permute-start.1) | collective-permute-done | bytes 524320 | tf_op jit(solution)/shard_map/ppermute | solution.py:17
  27.6 5.1 %fusion = bf16[64,32,128]{2,1,0:T(8,128)(2,1)S(1)} fusion(bf16[32,64,3,128]{3,0,2,1:T(8,128)(2,1)S(1)} %bitcast.123, bf16[64,3,128,128]{3,2,1,0:T(8,128)(2,1)} %param.23), kind=kOutput, calls=%fused_computation.17 | convolution fusion | flops 201588736 | bytes 8388608 | tf_op jit(solution)/shard_map/rkij,mrkj->mri/dot_general | solution.py:41
  32.7 1.9 collective-permute-start.3
  34.6 3.6 %collective-permute-start.2 = (bf16[32,8192]{1,0:T(8,128)(2,1)S(1)}, bf16[32,8192]{1,0:T(8,128)(2,1)S(1)}, u32[]{:S(2)}, u32[]{:S(2)}) collective-permute-start(bf16[32,8192]{1,0:T(8,128)(2,1)S(1)} %copy_bitcast_fusion.4), channel_id=1, source_target_pairs={{0,4},{4,8},{8,12},{12,16},{16,20},{20,24},{24,28},{1,5},{5,9},{9,... | collective-permute-start | bytes 1572872 | tf_op jit(solution)/shard_map/ppermute | solution.py:16
  38.6 6.4 %collective-permute-done.3 = bf16[32,8192]{1,0:T(8,128)(2,1)S(1)} collective-permute-done((bf16[32,8192]{1,0:T(8,128)(2,1)S(1)}, bf16[32,8192]{1,0:T(8,128)(2,1)S(1)}, u32[]{:S(2)}, u32[]{:S(2)}) %collective-permute-start.3) | collective-permute-done | bytes 524320 | tf_op jit(solution)/shard_map/ppermute | solution.py:17
  46.5 2.3 %gather_fusion.1 = bf16[192,32,128]{2,1,0:T(8,128)(2,1)S(1)} fusion(bf16[32,192,128]{2,0,1:T(8,128)(2,1)} %pad_maximum_fusion, s32[1024]{0:T(1024)S(1)} %pad_clamp_fusion), kind=kCustom, calls=%fused_computation.1 | custom fusion | bytes 3146496 | tf_op jit(solution)/shard_map/gather | solution.py:40
  48.9 5.1 %fusion.4 = (f32[64,128]{1,0:T(8,128)S(1)}, f32[64,128]{1,0:T(8,128)S(1)}, f32[32,64,128]{2,0,1:T(8,128)S(1)}) fusion(f32[32,64]{0,1:T(8,128)S(1)} %copy.44, bf16[64,32,128]{2,1,0:T(8,128)(2,1)S(1)} %fusion, bf16[32,64,3,128]{3,0,2,1:T(8,128)(2,1)S(1)} %bitcast.122, bf16[64,3,128,128]{3,2,1,0:T(8,128)(2,1)} %param.23), kind=kOutput, calls=%fused_computation.21 | convolution fusion | flops 203145216 | bytes 9510912 | tf_op jit(solution)/shard_map/rkij,mrkj->mri/dot_general | solution.py:41
  54.7 36.1 %all-reduce.2.cloned.1.call-done = f32[2,64,128]{2,1,0:T(8,128)} async-done(((f32[2,64,128]{2,1,0:T(8,128)}), f32[2,64,128]{2,1,0:T(8,128)}) %all-reduce.2.cloned.1.call-update) | async-done | bytes 65552 | tf_op jit(solution)/shard_map/psum | solution.py:75
  92.1 13.8 %psum.15 = f32[32]{0:T(128)S(1)} all-reduce(f32[32]{0:T(128)S(1)} %multiply_reduce_fusion.1), channel_id=1, replica_groups=mesh['space'=8,'members'=4] {'space'}, use_global_device_ids=true, to_apply=%region_7.0 | all-reduce | flops 32 | bytes 256 | tf_op jit(solution)/shard_map/psum | solution.py:86
  105.9 5.7 %fusion.13 = f32[64,32,3,128]{3,1,2,0:T(8,128)} fusion(bf16[64,3,128,128]{3,2,1,0:T(8,128)(2,1)} %param.23, f32[64,128]{1,0:T(8,128)S(1)} %get-tuple-element.99, f32[32,64]{0,1:T(8,128)S(1)} %get-tuple-element.101), kind=kOutput, calls=%fused_computation.36 | convolution fusion | flops 201850880 | bytes 9478144 | tf_op jit(solution)/shard_map/rkij,mri->mrkj/dot_general | solution.py:44
  112.0 17.3 %scatter_fusion = f32[32,192,128]{2,0,1:T(8,128)S(1)} fusion(f32[32,192,128]{2,0,1:T(8,128)S(1)} %broadcast.210.clone, s32[192]{0:T(256)S(1)} %bitcast.128, f32[192,32,128]{2,1,0:T(8,128)} %bitcast.119), kind=kCustom, calls=%fused_computation.2 | custom fusion | flops 786432 | bytes 9437952 | tf_op jit(solution)/shard_map/scatter-add | solution.py:48
  131.7 2.6 %collective-permute-start.5 = (f32[32,8192]{1,0:T(8,128)S(1)}, f32[32,8192]{1,0:T(8,128)S(1)}, u32[]{:S(2)}, u32[]{:S(2)}) collective-permute-start(f32[32,8192]{1,0:T(8,128)S(1)} %get-tuple-element.97), channel_id=1, source_target_pairs={{4,0},{8,4},{12,8},{16,12},{20,16},{24,20},{28,24},{5,1},{9,5},{13... | collective-permute-start | bytes 3145736 | tf_op jit(solution)/shard_map/ppermute | solution.py:17
  134.4 9.1 %collective-permute-done.4 = f32[32,8192]{1,0:T(8,128)S(1)} collective-permute-done((f32[32,8192]{1,0:T(8,128)S(1)}, f32[32,8192]{1,0:T(8,128)S(1)}, u32[]{:S(2)}, u32[]{:S(2)}) %collective-permute-start.4) | collective-permute-done | bytes 1048608 | tf_op jit(solution)/shard_map/ppermute | solution.py:16
  143.4 14.6 %collective-permute-done.5 = f32[32,8192]{1,0:T(8,128)S(1)} collective-permute-done((f32[32,8192]{1,0:T(8,128)S(1)}, f32[32,8192]{1,0:T(8,128)S(1)}, u32[]{:S(2)}, u32[]{:S(2)}) %collective-permute-start.5) | collective-permute-done | bytes 1048608 | tf_op jit(solution)/shard_map/ppermute | solution.py:17
  160.9 3.9 %fusion.16 = f32[64,32,3,128]{3,1,2,0:T(8,128)} fusion(bf16[64,3,128,128]{3,2,1,0:T(8,128)(2,1)S(1)} %bitcast.116, f32[32,64,128]{2,1,0:T(8,128)S(1)} %get-tuple-element.89, f32[32,64,128]{2,1,0:T(8,128)S(1)} %get-tuple-element.88, f32[32,192,128]{2,0,1:T(8,128)S(1)} %scatter_fusion, f32[64,128]{1,0:T(8,128)S(1)} %get-tuple-element.98, ...), kind=kOutput, calls=%fused_computation.38 | convolution fusion | flops 203161600 | bytes 12648448 | tf_op jit(solution)/shard_map/rkij,mri->mrkj/dot_general | solution.py:44
  165.2 17.3 %scatter_fusion.1 = f32[32,192,128]{2,0,1:T(8,128)S(1)} fusion(f32[32,192,128]{2,0,1:T(8,128)S(1)} %broadcast.210, s32[192]{0:T(256)S(1)} %bitcast.129, f32[192,32,128]{2,1,0:T(8,128)} %bitcast.118), kind=kCustom, calls=%fused_computation.3 | custom fusion | flops 786432 | bytes 9437952 | tf_op jit(solution)/shard_map/scatter-add | solution.py:48
  187.5 3.4 %collective-permute-start.7 = (f32[32,8192]{1,0:T(8,128)}, f32[32,8192]{1,0:T(8,128)}, u32[]{:S(2)}, u32[]{:S(2)}) collective-permute-start(f32[32,8192]{1,0:T(8,128)} %get-tuple-element.95), channel_id=1, source_target_pairs={{4,0},{8,4},{12,8},{16,12},{20,16},{24,20},{28,24},{5,1},{9,5},{13... | collective-permute-start | bytes 3145736 | tf_op jit(solution)/shard_map/ppermute | solution.py:17
  191.6 8.0 %collective-permute-done.6 = f32[32,8192]{1,0:T(8,128)} collective-permute-done((f32[32,8192]{1,0:T(8,128)}, f32[32,8192]{1,0:T(8,128)}, u32[]{:S(2)}, u32[]{:S(2)}) %collective-permute-start.6) | collective-permute-done | bytes 1048608 | tf_op jit(solution)/shard_map/ppermute | solution.py:16
  199.6 13.5 %collective-permute-done.7 = f32[32,8192]{1,0:T(8,128)} collective-permute-done((f32[32,8192]{1,0:T(8,128)}, f32[32,8192]{1,0:T(8,128)}, u32[]{:S(2)}, u32[]{:S(2)}) %collective-permute-start.7) | collective-permute-done | bytes 1048608 | tf_op jit(solution)/shard_map/ppermute | solution.py:17
  213.1 2.4 %maximum_bitcast_fusion.1 = f32[4,8,256,128]{3,1,2,0:T(8,128)S(1)} fusion(f32[32,8192]{1,0:T(8,128)} %collective-permute-done.7, f32[32,16384]{1,0:T(8,128)} %copy-done, f32[32,8192]{1,0:T(8,128)} %collective-permute-done.6), kind=kLoop, calls=%fused_computation.5 | loop fusion | flops 2097152 | bytes 8388608
  216.5 2.2 copy_bitcast_fusion.3
  (60 shorter events, 19.8 us)
Async XLA Ops:
  7.2 83.7 %all-reduce.2.cloned.1.call-start = ((), (), s32[]{:S(2)}) async-start(), calls=%async_computation | async-start | bytes 131072 | tf_op jit(solution)/shard_map/psum | solution.py:75
  7.2 10.9 %collective-permute-start = (bf16[32,8192]{1,0:T(8,128)(2,1)}, bf16[32,8192]{1,0:T(8,128)(2,1)S(1)}, u32[]{:S(2)}, u32[]{:S(2)}) collective-permute-start(bf16[32,8192]{1,0:T(8,128)(2,1)} %param.22), channel_id=1, source_target_pairs={{0,4},{4,8},{8,12},{12,16},{16,20},{20,24},{24,28},{1,5},{5,9},{9,... | collective-permute-start | bytes 1572872 | tf_op jit(solution)/shard_map/ppermute | solution.py:16
  11.7 13.6 %collective-permute-start.1 = (bf16[32,8192]{1,0:T(8,128)(2,1)}, bf16[32,8192]{1,0:T(8,128)(2,1)S(1)}, u32[]{:S(2)}, u32[]{:S(2)}) collective-permute-start(bf16[32,8192]{1,0:T(8,128)(2,1)} %param.22), channel_id=1, source_target_pairs={{4,0},{8,4},{12,8},{16,12},{20,16},{24,20},{28,24},{5,1},{9,5},{13... | collective-permute-start | bytes 1572872 | tf_op jit(solution)/shard_map/ppermute | solution.py:17
  27.5 10.7 %copy-start.4 = (s32[64,2]{0,1:T(2,128)S(1)}, s32[64,2]{0,1:T(2,128)}, u32[]{:S(2)}) copy-start(s32[64,2]{0,1:T(2,128)} %param.24) | copy-start | bytes 1540
  27.5 11.0 %copy-start.3 = (f32[32,64]{1,0:T(8,128)S(1)}, f32[32,64]{1,0:T(8,128)}, u32[]{:S(2)}) copy-start(f32[32,64]{1,0:T(8,128)} %param.25) | copy-start | bytes 24580
  32.7 12.3 %collective-permute-start.3 = (bf16[32,8192]{1,0:T(8,128)(2,1)S(1)}, bf16[32,8192]{1,0:T(8,128)(2,1)S(1)}, u32[]{:S(2)}, u32[]{:S(2)}) collective-permute-start(bf16[32,8192]{1,0:T(8,128)(2,1)S(1)} %copy_bitcast_fusion.4), channel_id=1, source_target_pairs={{4,0},{8,4},{12,8},{16,12},{20,16},{24,20},{28,24},{5,1},{9,5},{13... | collective-permute-start | bytes 1572872 | tf_op jit(solution)/shard_map/ppermute | solution.py:17
  34.6 10.5 %collective-permute-start.2 = (bf16[32,8192]{1,0:T(8,128)(2,1)S(1)}, bf16[32,8192]{1,0:T(8,128)(2,1)S(1)}, u32[]{:S(2)}, u32[]{:S(2)}) collective-permute-start(bf16[32,8192]{1,0:T(8,128)(2,1)S(1)} %copy_bitcast_fusion.4), channel_id=1, source_target_pairs={{0,4},{4,8},{8,12},{12,16},{16,20},{20,24},{24,28},{1,5},{5,9},{9,... | collective-permute-start | bytes 1572872 | tf_op jit(solution)/shard_map/ppermute | solution.py:16
  48.9 42.0 %copy-start.1 = (f32[2,8192]{1,0:T(2,128)S(1)}, f32[2,8192]{1,0:T(2,128)}, u32[]{:S(2)}) copy-start(f32[2,8192]{1,0:T(2,128)} %param.26) | copy-start | bytes 196612
  48.9 42.0 %copy-start.2 = (f32[2,8192]{1,0:T(2,128)S(1)}, f32[2,8192]{1,0:T(2,128)}, u32[]{:S(2)}) copy-start(f32[2,8192]{1,0:T(2,128)} %param.27) | copy-start | bytes 196612
  129.8 13.7 %collective-permute-start.4 = (f32[32,8192]{1,0:T(8,128)S(1)}, f32[32,8192]{1,0:T(8,128)S(1)}, u32[]{:S(2)}, u32[]{:S(2)}) collective-permute-start(f32[32,8192]{1,0:T(8,128)S(1)} %get-tuple-element.96), channel_id=1, source_target_pairs={{0,4},{4,8},{8,12},{12,16},{16,20},{20,24},{24,28},{1,5},{5,9},{9,... | collective-permute-start | bytes 3145736 | tf_op jit(solution)/shard_map/ppermute | solution.py:16
  131.7 26.3 %collective-permute-start.5 = (f32[32,8192]{1,0:T(8,128)S(1)}, f32[32,8192]{1,0:T(8,128)S(1)}, u32[]{:S(2)}, u32[]{:S(2)}) collective-permute-start(f32[32,8192]{1,0:T(8,128)S(1)} %get-tuple-element.97), channel_id=1, source_target_pairs={{4,0},{8,4},{12,8},{16,12},{20,16},{24,20},{28,24},{5,1},{9,5},{13... | collective-permute-start | bytes 3145736 | tf_op jit(solution)/shard_map/ppermute | solution.py:17
  158.0 1.6 slice-start
  158.3 2.6 %slice-start.1 = ((s8[6291456]{0:T(1024)(128)(4,1)}), s8[4194304]{0:T(1024)(128)(4,1)S(1)}, s32[]{:S(2)}) async-start(s8[6291456]{0:T(1024)(128)(4,1)} %bitcast.115), calls=%async_computation.2 | async-start | bytes 8388608
  182.8 1.3 copy-start
  185.6 14.0 %collective-permute-start.6 = (f32[32,8192]{1,0:T(8,128)}, f32[32,8192]{1,0:T(8,128)}, u32[]{:S(2)}, u32[]{:S(2)}) collective-permute-start(f32[32,8192]{1,0:T(8,128)} %get-tuple-element.94), channel_id=1, source_target_pairs={{0,4},{4,8},{8,12},{12,16},{16,20},{20,24},{24,28},{1,5},{5,9},{9,... | collective-permute-start | bytes 3145736 | tf_op jit(solution)/shard_map/ppermute | solution.py:16
  187.5 25.6 %collective-permute-start.7 = (f32[32,8192]{1,0:T(8,128)}, f32[32,8192]{1,0:T(8,128)}, u32[]{:S(2)}, u32[]{:S(2)}) collective-permute-start(f32[32,8192]{1,0:T(8,128)} %get-tuple-element.95), channel_id=1, source_target_pairs={{4,0},{8,4},{12,8},{16,12},{20,16},{24,20},{28,24},{5,1},{9,5},{13... | collective-permute-start | bytes 3145736 | tf_op jit(solution)/shard_map/ppermute | solution.py:17
Sparse Core Ops, SparseCore 0:
  54.8 35.9 all-reduce.1
where the time goes:
time: 227 us; the launch traced here: 226 us
  waiting for transfers between devices  98.3 us (43%)
  other arithmetic  45.1 us (20%)
  starting transfers between devices  21.9 us (10%)
  matrix products  19.8 us (9%)
  between operations  14.4 us (6%)
  blocking collectives  13.8 us (6%)
  local copies, waits for them, and re-layouts  12.3 us (5%)
    ppermute x4, waiting for transfers between devices, padded(): after = lax.ppermute(leading, axis, down)  41.6 us
    psum x1, waiting for transfers between devices, on_device(): increments = lax.psum(partial_sums, 'members') * member_scale  36.1 us
    scatter-add x2, other arithmetic, adjoint(): spread_rows.at[:, every_col.reshape(-1), :]  34.6 us
    ppermute x4, waiting for transfers between devices, padded(): before = lax.ppermute(last, axis, up)  20.6 us
    psum x1, blocking collectives, on_device(): squares = lax.psum(jnp.sum(grad_weights * grad_weights, axis=1), 'space')  13.8 us
    ppermute x4, starting transfers between devices, padded(): before = lax.ppermute(last, axis, up)  12 us
    dot_general x2, matrix products, forward(): jnp.einsum('rkij,mrkj->mri', op_blocks, picked, preferred_element_type=jn...  10.2 us
    ppermute x4, starting transfers between devices, padded(): after = lax.ppermute(leading, axis, down)  9.86 us
  transfers between devices with their start and end apart: 9, of which 8 were waited for; matrix products, arithmetic and copies ran while one was open for 1% of the time, Pallas kernels for 0%

commit v1 on v0

--- a/solution.py
+++ b/solution.py
@@ -72,7 +72,7 @@
     )
     observed = innovations.reshape(2, blocks, block_size)
     precision = obs_precision.reshape(2, blocks, block_size)
-    increments = lax.psum(partial_sums, "members") * member_scale
+    increments = jnp.sum(lax.all_gather(partial_sums, "members"), axis=0) * member_scale
     residual = precision * (increments - observed)
     cot_one = (member_scale * weight_col * residual[0][None]).astype(jnp.bfloat16)
     cot_two = (member_scale * weight_col * residual[1][None]).astype(jnp.bfloat16)

time: 227 us -> 193 us (0.85)
  waiting for transfers between devices: 98.3 us -> 63.7 us
  blocking collectives: 13.8 us -> 28.4 us
  between operations: 14.4 us -> 1.04 us
    psum x1 -> x0, waiting for transfers between devices: 36.1 us -> none  [on_device(): increments = lax.psum(partial_sums, 'members') * member_scale]
    all_gather x0 -> x1, blocking collectives: none -> 11.9 us  [on_device(): lax.all_gather(partial_sums, 'members')]
    psum x1, blocking collectives: 13.8 us -> 16.4 us  [on_device(): squares = lax.psum(jnp.sum(grad_weights * grad_weights, axis=1), 'space')]
  transfers between devices with their start and end apart: 9 -> 8, of which waited for: 8 -> 7; matrix products, arithmetic and copies ran while one was open for 1% -> 1% of each run, Pallas kernels for 0% -> 0%
where the time goes in v1:
time: 193 us; the launch traced here: 191 us
  waiting for transfers between devices  63.7 us (33%)
  other arithmetic  43.6 us (23%)
  blocking collectives  28.4 us (15%)
  starting transfers between devices  22.6 us (12%)
  matrix products  19.8 us (10%)
  local copies, waits for them, and re-layouts  12.3 us (6%)
    ppermute x4, waiting for transfers between devices, padded(): after = lax.ppermute(leading, axis, down)  42.6 us
    scatter-add x2, other arithmetic, adjoint(): spread_rows.at[:, every_col.reshape(-1), :]  34.6 us
    ppermute x4, waiting for transfers between devices, padded(): before = lax.ppermute(last, axis, up)  21.1 us
    psum x1, blocking collectives, on_device(): squares = lax.psum(jnp.sum(grad_weights * grad_weights, axis=1), 'space')  16.4 us
    ppermute x4, starting transfers between devices, padded(): before = lax.ppermute(last, axis, up)  13.2 us
    all_gather x1, blocking collectives, on_device(): lax.all_gather(partial_sums, 'members')  11.9 us
    dot_general x2, matrix products, forward(): jnp.einsum('rkij,mrkj->mri', op_blocks, picked, preferred_element_type=jn...  10.2 us
    dot_general x2, matrix products, adjoint(): jnp.einsum('rkij,mri->mrkj', op_blocks, cotangent, preferred_element_type...  9.58 us
  transfers between devices with their start and end apart: 8, of which 7 were waited for; matrix products, arithmetic and copies ran while one was open for 1% of the time, Pallas kernels for 0%

profile of v1, /device:TPU:1, one launch (start us, length us, event | category | flops | bytes accessed | tf_op | source)
XLA Modules:
  0.0 191.4 jit_solution(16111903901500904895)
XLA Ops:
  0.6 4.5 %collective-permute-start = (bf16[32,8192]{1,0:T(8,128)(2,1)}, bf16[32,8192]{1,0:T(8,128)(2,1)S(1)}, u32[]{:S(2)}, u32[]{:S(2)}) collective-permute-start(bf16[32,8192]{1,0:T(8,128)(2,1)} %param.22), channel_id=1, source_target_pairs={{0,4},{4,8},{8,12},{12,16},{16,20},{20,24},{24,28},{1,5},{5,9},{9,... | collective-permute-start | bytes 1572872 | tf_op jit(solution)/shard_map/ppermute | solution.py:16
  5.1 1.9 %collective-permute-start.1 = (bf16[32,8192]{1,0:T(8,128)(2,1)}, bf16[32,8192]{1,0:T(8,128)(2,1)S(1)}, u32[]{:S(2)}, u32[]{:S(2)}) collective-permute-start(bf16[32,8192]{1,0:T(8,128)(2,1)} %param.22), channel_id=1, source_target_pairs={{4,0},{8,4},{12,8},{16,12},{20,16},{24,20},{28,24},{5,1},{9,5},{13... | collective-permute-start | bytes 1572872 | tf_op jit(solution)/shard_map/ppermute | solution.py:17
  8.1 3.5 %collective-permute-done = bf16[32,8192]{1,0:T(8,128)(2,1)S(1)} collective-permute-done((bf16[32,8192]{1,0:T(8,128)(2,1)}, bf16[32,8192]{1,0:T(8,128)(2,1)S(1)}, u32[]{:S(2)}, u32[]{:S(2)}) %collective-permute-start) | collective-permute-done | bytes 524320 | tf_op jit(solution)/shard_map/ppermute | solution.py:16
  11.6 7.2 %collective-permute-done.1 = bf16[32,8192]{1,0:T(8,128)(2,1)S(1)} collective-permute-done((bf16[32,8192]{1,0:T(8,128)(2,1)}, bf16[32,8192]{1,0:T(8,128)(2,1)S(1)}, u32[]{:S(2)}, u32[]{:S(2)}) %collective-permute-start.1) | collective-permute-done | bytes 524320 | tf_op jit(solution)/shard_map/ppermute | solution.py:17
  21.0 5.1 %fusion = bf16[64,32,128]{2,1,0:T(8,128)(2,1)S(1)} fusion(bf16[32,64,3,128]{3,0,2,1:T(8,128)(2,1)S(1)} %bitcast.124, bf16[64,3,128,128]{3,2,1,0:T(8,128)(2,1)} %param.23), kind=kOutput, calls=%fused_computation.17 | convolution fusion | flops 201588736 | bytes 8388608 | tf_op jit(solution)/shard_map/rkij,mrkj->mri/dot_general | solution.py:41
  28.1 3.6 %collective-permute-start.2 = (bf16[32,8192]{1,0:T(8,128)(2,1)S(1)}, bf16[32,8192]{1,0:T(8,128)(2,1)S(1)}, u32[]{:S(2)}, u32[]{:S(2)}) collective-permute-start(bf16[32,8192]{1,0:T(8,128)(2,1)S(1)} %copy_bitcast_fusion.4), channel_id=1, source_target_pairs={{0,4},{4,8},{8,12},{12,16},{16,20},{20,24},{24,28},{1,5},{5,9},{9,... | collective-permute-start | bytes 1572872 | tf_op jit(solution)/shard_map/ppermute | solution.py:16
  32.1 6.3 %collective-permute-done.3 = bf16[32,8192]{1,0:T(8,128)(2,1)S(1)} collective-permute-done((bf16[32,8192]{1,0:T(8,128)(2,1)S(1)}, bf16[32,8192]{1,0:T(8,128)(2,1)S(1)}, u32[]{:S(2)}, u32[]{:S(2)}) %collective-permute-start.3) | collective-permute-done | bytes 524320 | tf_op jit(solution)/shard_map/ppermute | solution.py:17
  40.0 2.3 %gather_fusion.1 = bf16[192,32,128]{2,1,0:T(8,128)(2,1)S(1)} fusion(bf16[32,192,128]{2,0,1:T(8,128)(2,1)} %pad_maximum_fusion, s32[1024]{0:T(1024)S(1)} %pad_clamp_fusion), kind=kCustom, calls=%fused_computation.1 | custom fusion | bytes 3146496 | tf_op jit(solution)/shard_map/gather | solution.py:40
  42.3 5.1 %fusion.4 = (f32[64,128]{1,0:T(8,128)S(1)}, f32[64,128]{1,0:T(8,128)S(1)}, f32[32,64,128]{2,0,1:T(8,128)S(1)}) fusion(f32[32,64]{0,1:T(8,128)S(1)} %copy.44, bf16[64,32,128]{2,1,0:T(8,128)(2,1)S(1)} %fusion, bf16[32,64,3,128]{3,0,2,1:T(8,128)(2,1)S(1)} %bitcast.123, bf16[64,3,128,128]{3,2,1,0:T(8,128)(2,1)} %param.23), kind=kOutput, calls=%fused_computation.21 | convolution fusion | flops 203145216 | bytes 9510912 | tf_op jit(solution)/shard_map/rkij,mrkj->mri/dot_general | solution.py:41
  47.4 11.9 %all-gather = f32[8,64,128]{2,1,0:T(8,128)S(1)} all-gather(f32[2,64,128]{2,1,0:T(8,128)S(1)} %pad_maximum_fusion.1), channel_id=2, replica_groups=mesh['space'=8,'members'=4] {'members'}, dimensions={0}, use_global_device_ids=true | all-gather | bytes 327680 | tf_op jit(solution)/shard_map/all_gather | solution.py:75
  59.9 16.4 %psum.7 = f32[32]{0:T(128)S(1)} all-reduce(f32[32]{0:T(128)S(1)} %multiply_reduce_fusion.1), channel_id=1, replica_groups=mesh['space'=8,'members'=4] {'space'}, use_global_device_ids=true, to_apply=%region_7.0 | all-reduce | flops 32 | bytes 256 | tf_op jit(solution)/shard_map/psum | solution.py:86
  76.3 5.7 %fusion.13 = f32[64,32,3,128]{3,1,2,0:T(8,128)} fusion(bf16[64,3,128,128]{3,2,1,0:T(8,128)(2,1)} %param.23, f32[64,128]{1,0:T(8,128)S(1)} %get-tuple-element.99, f32[32,64]{0,1:T(8,128)S(1)} %get-tuple-element.101), kind=kOutput, calls=%fused_computation.36 | convolution fusion | flops 201850880 | bytes 9478144 | tf_op jit(solution)/shard_map/rkij,mri->mrkj/dot_general | solution.py:44
  82.4 17.3 %scatter_fusion = f32[32,192,128]{2,0,1:T(8,128)S(1)} fusion(f32[32,192,128]{2,0,1:T(8,128)S(1)} %broadcast.210.clone, s32[192]{0:T(256)S(1)} %bitcast.130, f32[192,32,128]{2,1,0:T(8,128)} %bitcast.120), kind=kCustom, calls=%fused_computation.2 | custom fusion | flops 786432 | bytes 9437952 | tf_op jit(solution)/shard_map/scatter-add | solution.py:48
  100.2 3.2 %collective-permute-start.4 = (f32[32,8192]{1,0:T(8,128)S(1)}, f32[32,8192]{1,0:T(8,128)S(1)}, u32[]{:S(2)}, u32[]{:S(2)}) collective-permute-start(f32[32,8192]{1,0:T(8,128)S(1)} %get-tuple-element.96), channel_id=1, source_target_pairs={{0,4},{4,8},{8,12},{12,16},{16,20},{20,24},{24,28},{1,5},{5,9},{9,... | collective-permute-start | bytes 3145736 | tf_op jit(solution)/shard_map/ppermute | solution.py:16
  103.4 2.1 %collective-permute-start.5 = (f32[32,8192]{1,0:T(8,128)S(1)}, f32[32,8192]{1,0:T(8,128)S(1)}, u32[]{:S(2)}, u32[]{:S(2)}) collective-permute-start(f32[32,8192]{1,0:T(8,128)S(1)} %get-tuple-element.97), channel_id=1, source_target_pairs={{4,0},{8,4},{12,8},{16,12},{20,16},{24,20},{28,24},{5,1},{9,5},{13... | collective-permute-start | bytes 3145736 | tf_op jit(solution)/shard_map/ppermute | solution.py:17
  105.5 9.6 %collective-permute-done.4 = f32[32,8192]{1,0:T(8,128)S(1)} collective-permute-done((f32[32,8192]{1,0:T(8,128)S(1)}, f32[32,8192]{1,0:T(8,128)S(1)}, u32[]{:S(2)}, u32[]{:S(2)}) %collective-permute-start.4) | collective-permute-done | bytes 1048608 | tf_op jit(solution)/shard_map/ppermute | solution.py:16
  115.1 15.0 %collective-permute-done.5 = f32[32,8192]{1,0:T(8,128)S(1)} collective-permute-done((f32[32,8192]{1,0:T(8,128)S(1)}, f32[32,8192]{1,0:T(8,128)S(1)}, u32[]{:S(2)}, u32[]{:S(2)}) %collective-permute-start.5) | collective-permute-done | bytes 1048608 | tf_op jit(solution)/shard_map/ppermute | solution.py:17
  133.0 3.9 %fusion.16 = f32[64,32,3,128]{3,1,2,0:T(8,128)} fusion(bf16[64,3,128,128]{3,2,1,0:T(8,128)(2,1)S(1)} %bitcast.117, f32[32,64,128]{2,1,0:T(8,128)S(1)} %get-tuple-element.89, f32[32,64,128]{2,1,0:T(8,128)S(1)} %get-tuple-element.88, f32[32,192,128]{2,0,1:T(8,128)S(1)} %scatter_fusion, f32[64,128]{1,0:T(8,128)S(1)} %get-tuple-element.98, ...), kind=kOutput, calls=%fused_computation.38 | convolution fusion | flops 203161600 | bytes 12648448 | tf_op jit(solution)/shard_map/rkij,mri->mrkj/dot_general | solution.py:44
  137.3 17.3 %scatter_fusion.1 = f32[32,192,128]{2,0,1:T(8,128)S(1)} fusion(f32[32,192,128]{2,0,1:T(8,128)S(1)} %broadcast.210, s32[192]{0:T(256)S(1)} %bitcast.131, f32[192,32,128]{2,1,0:T(8,128)} %bitcast.119), kind=kCustom, calls=%fused_computation.3 | custom fusion | flops 786432 | bytes 9437952 | tf_op jit(solution)/shard_map/scatter-add | solution.py:48
  159.6 3.4 %collective-permute-start.7 = (f32[32,8192]{1,0:T(8,128)}, f32[32,8192]{1,0:T(8,128)}, u32[]{:S(2)}, u32[]{:S(2)}) collective-permute-start(f32[32,8192]{1,0:T(8,128)} %get-tuple-element.95), channel_id=1, source_target_pairs={{4,0},{8,4},{12,8},{16,12},{20,16},{24,20},{28,24},{5,1},{9,5},{13... | collective-permute-start | bytes 3145736 | tf_op jit(solution)/shard_map/ppermute | solution.py:17
  163.7 8.0 %collective-permute-done.6 = f32[32,8192]{1,0:T(8,128)} collective-permute-done((f32[32,8192]{1,0:T(8,128)}, f32[32,8192]{1,0:T(8,128)}, u32[]{:S(2)}, u32[]{:S(2)}) %collective-permute-start.6) | collective-permute-done | bytes 1048608 | tf_op jit(solution)/shard_map/ppermute | solution.py:16
  171.7 14.0 %collective-permute-done.7 = f32[32,8192]{1,0:T(8,128)} collective-permute-done((f32[32,8192]{1,0:T(8,128)}, f32[32,8192]{1,0:T(8,128)}, u32[]{:S(2)}, u32[]{:S(2)}) %collective-permute-start.7) | collective-permute-done | bytes 1048608 | tf_op jit(solution)/shard_map/ppermute | solution.py:17
  185.7 2.4 %maximum_bitcast_fusion.1 = f32[4,8,256,128]{3,1,2,0:T(8,128)S(1)} fusion(f32[32,8192]{1,0:T(8,128)} %collective-permute-done.7, f32[32,16384]{1,0:T(8,128)} %copy-done, f32[32,8192]{1,0:T(8,128)} %collective-permute-done.6), kind=kLoop, calls=%fused_computation.5 | loop fusion | flops 2097152 | bytes 8388608
  189.2 2.2 %copy_bitcast_fusion.3 = f32[32,8192]{1,0:T(8,128)} fusion(f32[32,192,128]{2,0,1:T(8,128)S(1)} %scatter_fusion.1, f32[32,64,128]{2,1,0:T(8,128)S(1)} %get-tuple-element.87, f32[32,64,128]{2,1,0:T(8,128)S(1)} %get-tuple-element.86), kind=kLoop, calls=%fused_computation.24 | loop fusion | flops 524288 | bytes 4194304 | tf_op jit(solution)/shard_map/reshape | solution.py:80
  (59 shorter events, 18.3 us)
Async XLA Ops:
  0.6 10.9 %collective-permute-start = (bf16[32,8192]{1,0:T(8,128)(2,1)}, bf16[32,8192]{1,0:T(8,128)(2,1)S(1)}, u32[]{:S(2)}, u32[]{:S(2)}) collective-permute-start(bf16[32,8192]{1,0:T(8,128)(2,1)} %param.22), channel_id=1, source_target_pairs={{0,4},{4,8},{8,12},{12,16},{16,20},{20,24},{24,28},{1,5},{5,9},{9,... | collective-permute-start | bytes 1572872 | tf_op jit(solution)/shard_map/ppermute | solution.py:16
  5.1 13.6 %collective-permute-start.1 = (bf16[32,8192]{1,0:T(8,128)(2,1)}, bf16[32,8192]{1,0:T(8,128)(2,1)S(1)}, u32[]{:S(2)}, u32[]{:S(2)}) collective-permute-start(bf16[32,8192]{1,0:T(8,128)(2,1)} %param.22), channel_id=1, source_target_pairs={{4,0},{8,4},{12,8},{16,12},{20,16},{24,20},{28,24},{5,1},{9,5},{13... | collective-permute-start | bytes 1572872 | tf_op jit(solution)/shard_map/ppermute | solution.py:17
  21.0 7.1 %copy-start.4 = (s32[64,2]{0,1:T(2,128)S(1)}, s32[64,2]{0,1:T(2,128)}, u32[]{:S(2)}) copy-start(s32[64,2]{0,1:T(2,128)} %param.24) | copy-start | bytes 1540
  21.0 11.0 %copy-start.3 = (f32[32,64]{1,0:T(8,128)S(1)}, f32[32,64]{1,0:T(8,128)}, u32[]{:S(2)}) copy-start(f32[32,64]{1,0:T(8,128)} %param.25) | copy-start | bytes 24580
  26.1 12.3 %collective-permute-start.3 = (bf16[32,8192]{1,0:T(8,128)(2,1)S(1)}, bf16[32,8192]{1,0:T(8,128)(2,1)S(1)}, u32[]{:S(2)}, u32[]{:S(2)}) collective-permute-start(bf16[32,8192]{1,0:T(8,128)(2,1)S(1)} %copy_bitcast_fusion.4), channel_id=1, source_target_pairs={{4,0},{8,4},{12,8},{16,12},{20,16},{24,20},{28,24},{5,1},{9,5},{13... | collective-permute-start | bytes 1572872 | tf_op jit(solution)/shard_map/ppermute | solution.py:17
  28.1 10.4 %collective-permute-start.2 = (bf16[32,8192]{1,0:T(8,128)(2,1)S(1)}, bf16[32,8192]{1,0:T(8,128)(2,1)S(1)}, u32[]{:S(2)}, u32[]{:S(2)}) collective-permute-start(bf16[32,8192]{1,0:T(8,128)(2,1)S(1)} %copy_bitcast_fusion.4), channel_id=1, source_target_pairs={{0,4},{4,8},{8,12},{12,16},{16,20},{20,24},{24,28},{1,5},{5,9},{9,... | collective-permute-start | bytes 1572872 | tf_op jit(solution)/shard_map/ppermute | solution.py:16
  42.3 17.1 %copy-start.1 = (f32[2,8192]{1,0:T(2,128)S(1)}, f32[2,8192]{1,0:T(2,128)}, u32[]{:S(2)}) copy-start(f32[2,8192]{1,0:T(2,128)} %param.26) | copy-start | bytes 196612
  42.3 17.1 %copy-start.2 = (f32[2,8192]{1,0:T(2,128)S(1)}, f32[2,8192]{1,0:T(2,128)}, u32[]{:S(2)}) copy-start(f32[2,8192]{1,0:T(2,128)} %param.27) | copy-start | bytes 196612
  100.2 14.9 %collective-permute-start.4 = (f32[32,8192]{1,0:T(8,128)S(1)}, f32[32,8192]{1,0:T(8,128)S(1)}, u32[]{:S(2)}, u32[]{:S(2)}) collective-permute-start(f32[32,8192]{1,0:T(8,128)S(1)} %get-tuple-element.96), channel_id=1, source_target_pairs={{0,4},{4,8},{8,12},{12,16},{16,20},{20,24},{24,28},{1,5},{5,9},{9,... | collective-permute-start | bytes 3145736 | tf_op jit(solution)/shard_map/ppermute | solution.py:16
  103.4 26.8 %collective-permute-start.5 = (f32[32,8192]{1,0:T(8,128)S(1)}, f32[32,8192]{1,0:T(8,128)S(1)}, u32[]{:S(2)}, u32[]{:S(2)}) collective-permute-start(f32[32,8192]{1,0:T(8,128)S(1)} %get-tuple-element.97), channel_id=1, source_target_pairs={{4,0},{8,4},{12,8},{16,12},{20,16},{24,20},{28,24},{5,1},{9,5},{13... | collective-permute-start | bytes 3145736 | tf_op jit(solution)/shard_map/ppermute | solution.py:17
  130.1 1.6 slice-start
  130.4 2.6 %slice-start.1 = ((s8[6291456]{0:T(1024)(128)(4,1)}), s8[4194304]{0:T(1024)(128)(4,1)S(1)}, s32[]{:S(2)}) async-start(s8[6291456]{0:T(1024)(128)(4,1)} %bitcast.116), calls=%async_computation.1 | async-start | bytes 8388608
  154.9 1.3 copy-start
  157.7 14.0 %collective-permute-start.6 = (f32[32,8192]{1,0:T(8,128)}, f32[32,8192]{1,0:T(8,128)}, u32[]{:S(2)}, u32[]{:S(2)}) collective-permute-start(f32[32,8192]{1,0:T(8,128)} %get-tuple-element.94), channel_id=1, source_target_pairs={{0,4},{4,8},{8,12},{12,16},{16,20},{20,24},{24,28},{1,5},{5,9},{9,... | collective-permute-start | bytes 3145736 | tf_op jit(solution)/shard_map/ppermute | solution.py:16
  159.6 26.1 %collective-permute-start.7 = (f32[32,8192]{1,0:T(8,128)}, f32[32,8192]{1,0:T(8,128)}, u32[]{:S(2)}, u32[]{:S(2)}) collective-permute-start(f32[32,8192]{1,0:T(8,128)} %get-tuple-element.95), channel_id=1, source_target_pairs={{4,0},{8,4},{12,8},{16,12},{20,16},{24,20},{28,24},{5,1},{9,5},{13... | collective-permute-start | bytes 3145736 | tf_op jit(solution)/shard_map/ppermute | solution.py:17
